TPU v7x, 32 devices: a whole 2x2x4 slice. The times are simulated.
32 devices in a mesh: sim: 8 (over y, x, core), ana: 4 (over z).
Axes of the slice: x: 2, y: 2, z: 4, core: 2. Of those that a mesh axis runs over, the one named last changes fastest.
Arguments:
- initial_disp: float32 [256, 512, 128], P('ana', 'sim'), may hold values from -24 to 24
- initial_vel: float32 [256, 512, 128], P('ana', 'sim'), may hold values from -2 to 2
- stiffness: float32 [512, 128], P('sim'), may hold values from 0.05 to 0.35
- basis: float32 [512, 128, 512], P(('sim', 'ana')), may hold values from -5 to 5
- rotation: float32 [768, 512], replicated, may hold values from -0.21875 to 0.21875
Outputs:
- basis_out: float32 [512, 128, 512], P(('sim', 'ana'))
- coords: float32 [512, 256], replicated
All inputs are finite; a program needn't handle non-finite values.
Results may differ from a plain program's by a relative error of at most 0.000054.
Values sent between devices are 32-bit elements; how exact they have to be, the bound alone decides.
No kernel may reach another device: no remote copies, remote signals or barrier semaphores. Data moves between devices by JAX's collectives and lax.ppermute only.
A program may use at most 64 MiB of HBM per device.

v0:
```python
import math
import jax
import jax.numpy as jnp
from jax import lax
from jax.sharding import PartitionSpec as P

M = 256
K = 512
STEPS = 4
epsilon = 1e-06


def with_halo(value, sides, width):
    for axis, dim in sides:
        size, length = (lax.axis_size(axis), value.shape[dim])
        up = [(i, (i + 1) % size) for i in range(size - 1)]
        down = [(j, i) for i, j in up]
        last = lax.slice_in_dim(value, length - width, length, axis=dim)
        initial = lax.slice_in_dim(value, 0, width, axis=dim)
        before = lax.ppermute(last, axis, up)
        after = lax.ppermute(initial, axis, down)
        value = jnp.concatenate([before, value, after], axis=dim)
    return value


def accelerate(displace, stiffness):
    padded = with_halo(displace, (("sim", 1),), 1)
    padded = jnp.pad(padded, ((0, 0), (0, 0), (1, 1)))
    laplace = (
        padded[:, 2:, 1:-1]
        + padded[:, :-2, 1:-1]
        + padded[:, 1:-1, 2:]
        + padded[:, 1:-1, :-2]
        - 4.0 * displace
    )
    return stiffness[None] * (
        laplace - 0.5 * displace * displace * displace / (1.0 + displace * displace)
    )


def contract(left, right, left_dim, right_dim):
    return lax.dot_general(
        left,
        right,
        (((left_dim,), (right_dim,)), ((), ())),
        precision=lax.Precision.HIGHEST,
        preferred_element_type=jnp.float32,
    )


def per_device(initial_disp, initial_vel, stiffness, basis, rotation):
    displace = initial_disp
    velocity = initial_vel
    for step_index in range(STEPS):
        velocity = velocity + accelerate(displace, stiffness)
        displace = displace + velocity
    row_count = basis.shape[0] * basis.shape[1] * lax.axis_size("sim") * lax.axis_size("ana")
    basis_rows = basis.reshape(-1, K)
    totals = lax.psum(jnp.sum(displace * displace, axis=(1, 2)), "sim")
    member_scale = jnp.sqrt(totals / row_count + epsilon)
    outgoing = displace / member_scale[:, None, None]
    arrived = lax.all_to_all(outgoing, "ana", split_axis=1, concat_axis=0, tiled=True)
    unscaled = arrived.reshape(M, -1)
    coefficients = lax.psum(contract(basis_rows, unscaled, 0, 1), ("sim", "ana")) / row_count
    remainder = unscaled - contract(coefficients, basis_rows, 0, 1)
    gram_matrix = lax.psum(contract(remainder, remainder, 1, 1), ("sim", "ana")) / row_count
    factor = jnp.linalg.cholesky(gram_matrix)
    fresh_basis = jax.scipy.linalg.solve_triangular(factor, remainder, lower=True)
    top_rows = rotation[:K]
    bottom_rows = rotation[K:]
    basis_out = contract(basis_rows, top_rows, 1, 0) + contract(fresh_basis, bottom_rows, 0, 0)
    coords = (
        contract(top_rows, coefficients, 0, 0) + contract(bottom_rows, factor, 0, 1)
    ) * math.sqrt(K)
    return (basis_out.reshape(basis.shape), coords)


def solution(mesh):
    in_specs = (
        P("ana", "sim", None),
        P("ana", "sim", None),
        P("sim", None),
        P(("sim", "ana"), None, None),
        P(),
    )
    out_specs = (P(("sim", "ana"), None, None), P())
    return jax.shard_map(
        per_device, mesh=mesh, in_specs=in_specs, out_specs=out_specs, check_vma=False
    )
```

profile of v0, /device:TPU:0, one launch (start us, length us, event | category | flops | bytes accessed | tf_op | source)
XLA Modules:
  0.0 476.9 jit_solution(9723111592130537525)
XLA Ops:
  7.2 2.8 copy.23
  10.0 1.3 collective-permute-start
  11.4 3.3 collective-permute-start.1
  16.7 5.5 %copy_add_fusion = (f32[64,64,128]{2,0,1:T(8,128)S(1)}, f32[64,64,128]{2,0,1:T(8,128)S(1)}) fusion(f32[64,64,128]{2,1,0:T(8,128)S(1)} %copy-done.3, f32[64,64,128]{2,0,1:T(8,128)S(1)} %copy.23, f32[64,66,130]{2,0,1:T(8,128)S(1)} %select_maximum_fusion.6, f32[64,1,128]{2,0,1:T(8,128)S(1)} %collective-permute-done.1, ...), kind=kLoop, calls=%fused_computation.118 | loop fusion | flops 8912896 | bytes 14778368 | tf_op jit(solution)/shard_map/add | solution.py:56
  22.2 1.3 collective-permute-start.2
  23.5 5.3 %collective-permute-start.3 = (f32[64,1,128]{2,0,1:T(8,128)S(1)}, f32[64,1,128]{2,0,1:T(8,128)S(1)}, u32[]{:S(2)}, u32[]{:S(2)}) collective-permute-start(f32[64,1,128]{2,0,1:T(8,128)S(1)} %get-tuple-element.36), channel_id=1, source_target_pairs={{0,4},{4,8},{8,12},{12,16},{16,20},{20,24},{24,28},{1,5},{5,9},{9,... | collective-permute-start | bytes 98312 | tf_op jit(solution)/shard_map/ppermute | solution.py:20
  30.8 1.9 fusion.67
  32.7 1.3 collective-permute-start.4
  34.0 5.0 %collective-permute-start.5 = (f32[64,1,128]{2,0,1:T(8,128)S(1)}, f32[64,1,128]{2,0,1:T(8,128)S(1)}, u32[]{:S(2)}, u32[]{:S(2)}) collective-permute-start(f32[64,1,128]{2,0,1:T(8,128)S(1)} %get-tuple-element.34), channel_id=1, source_target_pairs={{0,4},{4,8},{8,12},{12,16},{16,20},{20,24},{24,28},{1,5},{5,9},{9,... | collective-permute-start | bytes 98312 | tf_op jit(solution)/shard_map/ppermute | solution.py:20
  41.1 1.8 fusion.65
  42.9 1.3 collective-permute-start.6
  44.2 5.0 %collective-permute-start.7 = (f32[64,1,128]{2,0,1:T(8,128)S(1)}, f32[64,1,128]{2,0,1:T(8,128)S(1)}, u32[]{:S(2)}, u32[]{:S(2)}) collective-permute-start(f32[64,1,128]{2,0,1:T(8,128)S(1)} %get-tuple-element.32), channel_id=1, source_target_pairs={{0,4},{4,8},{8,12},{12,16},{16,20},{20,24},{24,28},{1,5},{5,9},{9,... | collective-permute-start | bytes 98312 | tf_op jit(solution)/shard_map/ppermute | solution.py:20
  51.3 2.0 multiply_reduce_fusion
  53.3 17.1 %psum.21 = f32[64]{0:T(128)S(1)} all-reduce(f32[64]{0:T(128)S(1)} %get-tuple-element.22), channel_id=1, replica_groups=mesh['sim'=8,'ana'=4] {'sim'}, use_global_device_ids=true, to_apply=%region_1.2 | all-reduce | flops 64 | bytes 512 | tf_op jit(solution)/shard_map/psum | solution.py:59
  70.7 53.3 %all_to_all.15 = f32[64,64,128]{2,0,1:T(8,128)S(1)} all-to-all(f32[64,64,128]{2,0,1:T(8,128)S(1)} %broadcast_divide_fusion), channel_id=1, replica_groups=mesh['sim'=8,'ana'=4] {'ana'}, dimensions={1} | all-to-all | bytes 4194304 | tf_op jit(solution)/shard_map/all_to_all | solution.py:62
  124.0 1.2 copy.24
  125.3 1.3 copy-done.2
  126.6 4.9 %fusion.34 = f32[512,256]{0,1:T(8,128)} fusion(f32[2048,512]{1,0:T(8,128)S(1)} %bitcast.54, f32[32,8,16,128]{3,2,1,0:T(8,128)S(1)} %bitcast.55), kind=kOutput, calls=%fused_computation.71 | convolution fusion | flops 3221225472 | bytes 6815744 | tf_op jit(solution)/shard_map/dot_general | solution.py:42
  131.5 128.3 %all-reduce.8.cloned.1.call-done = f32[512,256]{0,1:T(8,128)} async-done(((f32[512,256]{0,1:T(8,128)}), f32[512,256]{0,1:T(8,128)}) %all-reduce.8.cloned.1.call-update) | async-done | bytes 524304 | tf_op jit(solution)/shard_map/psum | solution.py:64
  259.9 7.1 %convolution_subtract_fusion = f32[256,2048]{1,0:T(8,128)S(1)} fusion(f32[2048,512]{1,0:T(8,128)} %bitcast.52, f32[32,8,16,128]{3,2,1,0:T(8,128)} %bitcast.56, f32[512,256]{0,1:T(8,128)} %all-reduce.8.cloned.1.call-done), kind=kOutput, calls=%fused_computation.18 | convolution fusion | flops 3221880832 | bytes 8912896 | tf_op jit(solution)/shard_map/dot_general | solution.py:42
  267.0 2.6 fusion.75
  269.6 10.3 %fusion.40 = f32[2048,512]{1,0:T(8,128)} fusion(f32[2048,512]{1,0:T(8,128)} %bitcast.53, f32[768,512]{1,0:T(8,128)} %param.9), kind=kOutput, calls=%fused_computation.77 | convolution fusion | flops 6442450944 | bytes 9437184 | tf_op jit(solution)/shard_map/dot_general | solution.py:42
  279.9 113.8 %all-reduce.10.cloned.1.call-done = f32[256,256]{0,1:T(8,128)} async-done(((f32[256,256]{0,1:T(8,128)}), f32[256,256]{0,1:T(8,128)}) %all-reduce.10.cloned.1.call-update) | async-done | bytes 262160 | tf_op jit(solution)/shard_map/psum | solution.py:66
  395.8 11.7 %cholesky.50 = f32[128,128]{1,0:T(8,128)S(1)} custom-call(f32[128,128]{1,0:T(8,128)S(1)} %cholesky.118), custom_call_target="Cholesky" | custom-call | tf_op jit(solution)/shard_map/jit(cholesky)/cholesky | solution.py:67
  407.6 9.8 %custom-call.15 = f32[1,128,128]{1,2,0:T(8,128)S(1)} custom-call(f32[1,128,128]{2,1,0:T(8,128)S(1)} %get-tuple-element.43), custom_call_target="InvertDiagBlocksLowerTriangular" | custom-call | tf_op jit(solution)/shard_map/jit(cholesky)/cholesky | solution.py:67
  417.9 11.7 %cholesky.105 = f32[128,128]{1,0:T(8,128)S(1)} custom-call(f32[128,128]{1,0:T(8,128)S(1)} %convolution_subtract_fusion.2), custom_call_target="Cholesky" | custom-call | tf_op jit(solution)/shard_map/jit(cholesky)/cholesky | solution.py:67
  431.7 1.8 fusion.42
  436.3 4.0 while.1
  437.2 1.3 bitcast_dynamic-update-slice_fusion.2
  439.1 1.3 bitcast_dynamic-update-slice_fusion.2
  440.4 19.7 %custom-call.16 = f32[2,128,128]{1,2,0:T(8,128)S(1)} custom-call(f32[2,128,128]{2,1,0:T(8,128)S(1)} %get-tuple-element.9), custom_call_target="InvertDiagBlocksLowerTriangular" | custom-call | tf_op jit(solution)/shard_map/jit(_solve_triangular)/triangular_solve | solution.py:68
  463.3 6.3 %convolution_add_fusion = f32[2048,512]{1,0:T(8,128)} fusion(f32[2048,512]{1,0:T(8,128)S(1)} %copy-done.1, f32[128,2048]{1,0:T(8,128)S(1)} %fusion.55, f32[128,2048]{1,0:T(8,128)S(1)} %fusion.37, f32[768,512]{1,0:T(8,128)} %param.9), kind=kOutput, calls=%fused_computation.13 | convolution fusion | flops 3222798336 | bytes 11010048 | tf_op jit(solution)/shard_map/dot_general | solution.py:42
  (62 shorter events, 19.2 us)
Async XLA Ops:
  7.2 252.7 %all-reduce.8.cloned.1.call-start = ((), (), s32[]{:S(2)}) async-start(), calls=%async_computation.1 | async-start | bytes 1048576 | tf_op jit(solution)/shard_map/psum | solution.py:64
  10.0 4.6 collective-permute-start
  11.3 5.4 %copy-start.3 = (f32[64,64,128]{2,1,0:T(8,128)S(1)}, f32[64,64,128]{2,1,0:T(8,128)}, u32[]{:S(2)}) copy-start(f32[64,64,128]{2,1,0:T(8,128)} %param.5) | copy-start | bytes 6291460
  11.3 5.4 %copy-start.5 = (f32[64,64,128]{2,1,0:T(8,128)S(1)}, f32[64,64,128]{2,1,0:T(8,128)}, u32[]{:S(2)}) copy-start(f32[64,64,128]{2,1,0:T(8,128)} %param.6) | copy-start | bytes 6291460
  11.4 5.4 %copy-start.8 = (f32[64,128]{1,0:T(8,128)S(1)}, f32[64,128]{1,0:T(8,128)}, u32[]{:S(2)}) copy-start(f32[64,128]{1,0:T(8,128)} %param.7) | copy-start | bytes 98308
  11.4 4.1 collective-permute-start.1
  22.2 6.6 %collective-permute-start.2 = (f32[64,1,128]{2,0,1:T(8,128)S(1)}, f32[64,1,128]{2,0,1:T(8,128)S(1)}, u32[]{:S(2)}, u32[]{:S(2)}) collective-permute-start(f32[64,1,128]{2,0,1:T(8,128)S(1)} %get-tuple-element.37), channel_id=1, source_target_pairs={{4,0},{8,4},{12,8},{16,12},{20,16},{24,20},{28,24},{5,1},{9,5},{13... | collective-permute-start | bytes 98312 | tf_op jit(solution)/shard_map/ppermute | solution.py:21
  23.5 6.1 %collective-permute-start.3 = (f32[64,1,128]{2,0,1:T(8,128)S(1)}, f32[64,1,128]{2,0,1:T(8,128)S(1)}, u32[]{:S(2)}, u32[]{:S(2)}) collective-permute-start(f32[64,1,128]{2,0,1:T(8,128)S(1)} %get-tuple-element.36), channel_id=1, source_target_pairs={{0,4},{4,8},{8,12},{12,16},{16,20},{20,24},{24,28},{1,5},{5,9},{9,... | collective-permute-start | bytes 98312 | tf_op jit(solution)/shard_map/ppermute | solution.py:20
  32.7 6.3 %collective-permute-start.4 = (f32[64,1,128]{2,0,1:T(8,128)S(1)}, f32[64,1,128]{2,0,1:T(8,128)S(1)}, u32[]{:S(2)}, u32[]{:S(2)}) collective-permute-start(f32[64,1,128]{2,0,1:T(8,128)S(1)} %get-tuple-element.35), channel_id=1, source_target_pairs={{4,0},{8,4},{12,8},{16,12},{20,16},{24,20},{28,24},{5,1},{9,5},{13... | collective-permute-start | bytes 98312 | tf_op jit(solution)/shard_map/ppermute | solution.py:21
  34.0 5.9 %collective-permute-start.5 = (f32[64,1,128]{2,0,1:T(8,128)S(1)}, f32[64,1,128]{2,0,1:T(8,128)S(1)}, u32[]{:S(2)}, u32[]{:S(2)}) collective-permute-start(f32[64,1,128]{2,0,1:T(8,128)S(1)} %get-tuple-element.34), channel_id=1, source_target_pairs={{0,4},{4,8},{8,12},{12,16},{16,20},{20,24},{24,28},{1,5},{5,9},{9,... | collective-permute-start | bytes 98312 | tf_op jit(solution)/shard_map/ppermute | solution.py:20
  42.9 6.3 %collective-permute-start.6 = (f32[64,1,128]{2,0,1:T(8,128)S(1)}, f32[64,1,128]{2,0,1:T(8,128)S(1)}, u32[]{:S(2)}, u32[]{:S(2)}) collective-permute-start(f32[64,1,128]{2,0,1:T(8,128)S(1)} %get-tuple-element.33), channel_id=1, source_target_pairs={{4,0},{8,4},{12,8},{16,12},{20,16},{24,20},{28,24},{5,1},{9,5},{13... | collective-permute-start | bytes 98312 | tf_op jit(solution)/shard_map/ppermute | solution.py:21
  44.2 5.9 %collective-permute-start.7 = (f32[64,1,128]{2,0,1:T(8,128)S(1)}, f32[64,1,128]{2,0,1:T(8,128)S(1)}, u32[]{:S(2)}, u32[]{:S(2)}) collective-permute-start(f32[64,1,128]{2,0,1:T(8,128)S(1)} %get-tuple-element.32), channel_id=1, source_target_pairs={{0,4},{4,8},{8,12},{12,16},{16,20},{20,24},{24,28},{1,5},{5,9},{9,... | collective-permute-start | bytes 98312 | tf_op jit(solution)/shard_map/ppermute | solution.py:20
  124.0 2.5 copy-start
  125.3 1.3 copy-start.2
  131.5 262.1 %all-reduce.10.cloned.1.call-start = ((), (), s32[]{:S(2)}) async-start(), calls=%async_computation.2 | async-start | bytes 524288 | tf_op jit(solution)/shard_map/psum | solution.py:66
  394.6 39.6 %copy-start.6 = (f32[512,256]{0,1:T(8,128)S(1)}, f32[512,256]{0,1:T(8,128)}, u32[]{:S(2)}) copy-start(f32[512,256]{0,1:T(8,128)} %all-reduce.8.cloned.1.call-done) | copy-start | bytes 1572868
  431.6 2.6 copy-start.4
  434.2 2.1 copy-start.7
  461.1 2.2 copy-start.1
Sparse Core Ops, SparseCore 0:
  131.6 128.2 all-reduce.7
  269.7 123.9 all-reduce.9
where the time goes:
time: 486 us; the launch traced here: 477 us
  waiting for transfers between devices  245 us (50%)
  other arithmetic  72.6 us (15%)
  blocking collectives  70.4 us (14%)
  matrix products  37.5 us (8%)
  starting transfers between devices  23.8 us (5%)
  between operations  16.2 us (3%)
  local copies, waits for them, and re-layouts  10.5 us (2%)
    psum x1, waiting for transfers between devices, per_device(): lax.psum(contract(basis_rows, unscaled, 0, 1), ('sim', 'ana')) / row_count  128 us
    psum x1, waiting for transfers between devices, per_device(): lax.psum(contract(remainder, remainder, 1, 1), ('sim', 'ana')) / row_count  114 us
    all_to_all x1, blocking collectives, per_device(): lax.all_to_all(outgoing, 'ana', split_axis=1, concat_axis=0, tiled=True)  53.3 us
    another operation x6, other arithmetic, per_device(): factor = jnp.linalg.cholesky(gram_matrix)  34 us
    dot_general x7, matrix products, contract(): lax.dot_general(left, right, (((left_dim,), (right_dim,)), ((), ())), pre...  33.9 us
    another operation x3, other arithmetic, per_device(): jax.scipy.linalg.solve_triangular(factor, remainder, lower=True)  20.4 us
    ppermute x4, starting transfers between devices, with_halo(): before = lax.ppermute(last, axis, up)  18.6 us
    psum x1, blocking collectives, per_device(): totals = lax.psum(jnp.sum(displace * displace, axis=(1, 2)), 'sim')  17.1 us
  transfers between devices with their start and end apart: 10, of which 6 were waited for; matrix products, arithmetic and copies ran while one was open for 2% of the time, Pallas kernels for 0%

commit v1 on v0

--- a/solution.py
+++ b/solution.py
@@ -63,7 +63,7 @@
     unscaled = arrived.reshape(M, -1)
     coefficients = lax.psum(contract(basis_rows, unscaled, 0, 1), ("sim", "ana")) / row_count
     remainder = unscaled - contract(coefficients, basis_rows, 0, 1)
-    gram_matrix = lax.psum(contract(remainder, remainder, 1, 1), ("sim", "ana")) / row_count
+    gram_matrix = lax.psum(lax.psum(contract(remainder, remainder, 1, 1), "ana"), "sim") / row_count
     factor = jnp.linalg.cholesky(gram_matrix)
     fresh_basis = jax.scipy.linalg.solve_triangular(factor, remainder, lower=True)
     top_rows = rotation[:K]

time: 486 us -> 455 us (0.936)
  waiting for transfers between devices: 245 us -> 212 us
    psum x1 -> x2, waiting for transfers between devices: 114 us -> 80.5 us  [the longest x1 46.1 us: per_device(): lax.psum(lax.psum(contract(remainder, remainder, 1, 1), 'ana'), 'sim')]
  transfers between devices with their start and end apart: 10 -> 11, of which waited for: 6 -> 7; matrix products, arithmetic and copies ran while one was open for 2% -> 2% of each run, Pallas kernels for 0% -> 0%
where the time goes in v1:
time: 455 us; the launch traced here: 446 us
  waiting for transfers between devices  212 us (47%)
  other arithmetic  75.3 us (17%)
  blocking collectives  70.4 us (15%)
  matrix products  37.6 us (8%)
  starting transfers between devices  23.9 us (5%)
  between operations  15.9 us (3%)
  local copies, waits for them, and re-layouts  10.2 us (2%)
    psum x1, waiting for transfers between devices, per_device(): lax.psum(contract(basis_rows, unscaled, 0, 1), ('sim', 'ana')) / row_count  128 us
    all_to_all x1, blocking collectives, per_device(): lax.all_to_all(outgoing, 'ana', split_axis=1, concat_axis=0, tiled=True)  53.3 us
    psum x1, waiting for transfers between devices, per_device(): lax.psum(lax.psum(contract(remainder, remainder, 1, 1), 'ana'), 'sim')  46.1 us
    psum x1, waiting for transfers between devices, per_device(): lax.psum(contract(remainder, remainder, 1, 1), 'ana')  34.4 us
    dot_general x7, matrix products, contract(): lax.dot_general(left, right, (((left_dim,), (right_dim,)), ((), ())), pre...  34.1 us
    another operation x6, other arithmetic, per_device(): factor = jnp.linalg.cholesky(gram_matrix)  34 us
    another operation x3, other arithmetic, per_device(): jax.scipy.linalg.solve_triangular(factor, remainder, lower=True)  20.4 us
    ppermute x4, starting transfers between devices, with_halo(): before = lax.ppermute(last, axis, up)  18.6 us
  transfers between devices with their start and end apart: 11, of which 7 were waited for; matrix products, arithmetic and copies ran while one was open for 2% of the time, Pallas kernels for 0%

profile of v1, /device:TPU:0, one launch (start us, length us, event | category | flops | bytes accessed | tf_op | source)
XLA Modules:
  0.0 445.8 jit_solution(5110385182406980928)
XLA Ops:
  7.2 2.8 copy.23
  10.0 1.3 collective-permute-start
  11.4 3.3 collective-permute-start.1
  16.7 5.5 %copy_add_fusion = (f32[64,64,128]{2,0,1:T(8,128)S(1)}, f32[64,64,128]{2,0,1:T(8,128)S(1)}) fusion(f32[64,64,128]{2,1,0:T(8,128)S(1)} %copy-done.3, f32[64,64,128]{2,0,1:T(8,128)S(1)} %copy.23, f32[64,66,130]{2,0,1:T(8,128)S(1)} %select_maximum_fusion.6, f32[64,1,128]{2,0,1:T(8,128)S(1)} %collective-permute-done.1, ...), kind=kLoop, calls=%fused_computation.118 | loop fusion | flops 8912896 | bytes 14778368 | tf_op jit(solution)/shard_map/add | solution.py:56
  22.2 1.3 collective-permute-start.2
  23.5 5.3 %collective-permute-start.3 = (f32[64,1,128]{2,0,1:T(8,128)S(1)}, f32[64,1,128]{2,0,1:T(8,128)S(1)}, u32[]{:S(2)}, u32[]{:S(2)}) collective-permute-start(f32[64,1,128]{2,0,1:T(8,128)S(1)} %get-tuple-element.36), channel_id=1, source_target_pairs={{0,4},{4,8},{8,12},{12,16},{16,20},{20,24},{24,28},{1,5},{5,9},{9,... | collective-permute-start | bytes 98312 | tf_op jit(solution)/shard_map/ppermute | solution.py:20
  30.8 1.9 fusion.67
  32.8 1.3 collective-permute-start.4
  34.1 5.0 %collective-permute-start.5 = (f32[64,1,128]{2,0,1:T(8,128)S(1)}, f32[64,1,128]{2,0,1:T(8,128)S(1)}, u32[]{:S(2)}, u32[]{:S(2)}) collective-permute-start(f32[64,1,128]{2,0,1:T(8,128)S(1)} %get-tuple-element.34), channel_id=1, source_target_pairs={{0,4},{4,8},{8,12},{12,16},{16,20},{20,24},{24,28},{1,5},{5,9},{9,... | collective-permute-start | bytes 98312 | tf_op jit(solution)/shard_map/ppermute | solution.py:20
  41.1 1.8 fusion.65
  43.0 1.3 collective-permute-start.6
  44.3 5.0 %collective-permute-start.7 = (f32[64,1,128]{2,0,1:T(8,128)S(1)}, f32[64,1,128]{2,0,1:T(8,128)S(1)}, u32[]{:S(2)}, u32[]{:S(2)}) collective-permute-start(f32[64,1,128]{2,0,1:T(8,128)S(1)} %get-tuple-element.32), channel_id=1, source_target_pairs={{0,4},{4,8},{8,12},{12,16},{16,20},{20,24},{24,28},{1,5},{5,9},{9,... | collective-permute-start | bytes 98312 | tf_op jit(solution)/shard_map/ppermute | solution.py:20
  51.3 3.0 multiply_reduce_fusion
  54.3 17.1 %psum.28 = f32[64]{0:T(128)S(1)} all-reduce(f32[64]{0:T(128)S(1)} %get-tuple-element.22), channel_id=1, replica_groups=mesh['sim'=8,'ana'=4] {'sim'}, use_global_device_ids=true, to_apply=%region_1.2 | all-reduce | flops 64 | bytes 512 | tf_op jit(solution)/shard_map/psum | solution.py:59
  71.5 2.0 broadcast_divide_fusion
  73.4 53.3 %all_to_all.15 = f32[64,64,128]{2,0,1:T(8,128)S(1)} all-to-all(f32[64,64,128]{2,0,1:T(8,128)S(1)} %broadcast_divide_fusion), channel_id=1, replica_groups=mesh['sim'=8,'ana'=4] {'ana'}, dimensions={1} | all-to-all | bytes 4194304 | tf_op jit(solution)/shard_map/all_to_all | solution.py:62
  129.0 5.1 %fusion.34 = f32[512,256]{0,1:T(8,128)} fusion(f32[2048,512]{1,0:T(8,128)S(1)} %bitcast.54, f32[32,8,16,128]{3,2,1,0:T(8,128)S(1)} %bitcast.55), kind=kOutput, calls=%fused_computation.71 | convolution fusion | flops 3221225472 | bytes 6815744 | tf_op jit(solution)/shard_map/dot_general | solution.py:42
  134.1 128.3 %all-reduce.9.cloned.1.call-done = f32[512,256]{0,1:T(8,128)} async-done(((f32[512,256]{0,1:T(8,128)}), f32[512,256]{0,1:T(8,128)}) %all-reduce.9.cloned.1.call-update) | async-done | bytes 524304 | tf_op jit(solution)/shard_map/psum | solution.py:64
  262.4 7.1 %convolution_subtract_fusion = f32[256,2048]{1,0:T(8,128)S(1)} fusion(f32[2048,512]{1,0:T(8,128)} %bitcast.52, f32[32,8,16,128]{3,2,1,0:T(8,128)} %bitcast.56, f32[512,256]{0,1:T(8,128)} %all-reduce.9.cloned.1.call-done), kind=kOutput, calls=%fused_computation.18 | convolution fusion | flops 3221880832 | bytes 8912896 | tf_op jit(solution)/shard_map/dot_general | solution.py:42
  269.5 2.6 fusion.75
  272.2 34.4 %all-reduce.11.cloned.1.call-done = f32[256,256]{0,1:T(8,128)} async-done(((f32[256,256]{0,1:T(8,128)}), f32[256,256]{0,1:T(8,128)}) %all-reduce.11.cloned.1.call-update) | async-done | bytes 262160 | tf_op jit(solution)/shard_map/psum | solution.py:66
  306.6 10.3 %fusion.40 = f32[2048,512]{1,0:T(8,128)} fusion(f32[2048,512]{1,0:T(8,128)} %bitcast.53, f32[768,512]{1,0:T(8,128)} %param.9), kind=kOutput, calls=%fused_computation.77 | convolution fusion | flops 6442450944 | bytes 9437184 | tf_op jit(solution)/shard_map/dot_general | solution.py:42
  316.9 46.1 %all-reduce.13.cloned.1.call-done = f32[256,256]{0,1:T(8,128)} async-done(((f32[256,256]{0,1:T(8,128)}), f32[256,256]{0,1:T(8,128)}) %all-reduce.13.cloned.1.call-update) | async-done | bytes 262160 | tf_op jit(solution)/shard_map/psum | solution.py:66
  365.1 11.7 %cholesky.50 = f32[128,128]{1,0:T(8,128)S(1)} custom-call(f32[128,128]{1,0:T(8,128)S(1)} %cholesky.118), custom_call_target="Cholesky" | custom-call | tf_op jit(solution)/shard_map/jit(cholesky)/cholesky | solution.py:67
  376.9 9.8 %custom-call.15 = f32[1,128,128]{1,2,0:T(8,128)S(1)} custom-call(f32[1,128,128]{2,1,0:T(8,128)S(1)} %get-tuple-element.43), custom_call_target="InvertDiagBlocksLowerTriangular" | custom-call | tf_op jit(solution)/shard_map/jit(cholesky)/cholesky | solution.py:67
  387.2 11.7 %cholesky.105 = f32[128,128]{1,0:T(8,128)S(1)} custom-call(f32[128,128]{1,0:T(8,128)S(1)} %convolution_subtract_fusion.2), custom_call_target="Cholesky" | custom-call | tf_op jit(solution)/shard_map/jit(cholesky)/cholesky | solution.py:67
  401.0 1.8 fusion.42
  405.7 4.0 while.1
  406.5 1.3 bitcast_dynamic-update-slice_fusion.2
  408.4 1.3 bitcast_dynamic-update-slice_fusion.2
  409.7 19.7 %custom-call.16 = f32[2,128,128]{1,2,0:T(8,128)S(1)} custom-call(f32[2,128,128]{2,1,0:T(8,128)S(1)} %get-tuple-element.9), custom_call_target="InvertDiagBlocksLowerTriangular" | custom-call | tf_op jit(solution)/shard_map/jit(_solve_triangular)/triangular_solve | solution.py:68
  432.6 6.2 %convolution_add_fusion = f32[2048,512]{1,0:T(8,128)} fusion(f32[2048,512]{1,0:T(8,128)S(1)} %copy-done.1, f32[128,2048]{1,0:T(8,128)S(1)} %fusion.55, f32[128,2048]{1,0:T(8,128)S(1)} %fusion.37, f32[768,512]{1,0:T(8,128)} %param.9), kind=kOutput, calls=%fused_computation.13 | convolution fusion | flops 3222798336 | bytes 11010048 | tf_op jit(solution)/shard_map/dot_general | solution.py:42
  (65 shorter events, 21.2 us)
Async XLA Ops:
  7.2 255.3 %all-reduce.9.cloned.1.call-start = ((), (), s32[]{:S(2)}) async-start(), calls=%async_computation.1 | async-start | bytes 1048576 | tf_op jit(solution)/shard_map/psum | solution.py:64
  10.0 4.6 %collective-permute-start = (f32[64,1,128]{2,0,1:T(8,128)S(1)}, f32[64,1,128]{2,0,1:T(8,128)S(1)}, u32[]{:S(2)}, u32[]{:S(2)}) collective-permute-start(f32[64,1,128]{2,0,1:T(8,128)S(1)} %get-tuple-element.39), channel_id=1, source_target_pairs={{4,0},{8,4},{12,8},{16,12},{20,16},{24,20},{28,24},{5,1},{9,5},{13... | collective-permute-start | bytes 98312 | tf_op jit(solution)/shard_map/ppermute | solution.py:21
  11.3 5.4 %copy-start.3 = (f32[64,64,128]{2,1,0:T(8,128)S(1)}, f32[64,64,128]{2,1,0:T(8,128)}, u32[]{:S(2)}) copy-start(f32[64,64,128]{2,1,0:T(8,128)} %param.5) | copy-start | bytes 6291460
  11.3 5.4 %copy-start.5 = (f32[64,64,128]{2,1,0:T(8,128)S(1)}, f32[64,64,128]{2,1,0:T(8,128)}, u32[]{:S(2)}) copy-start(f32[64,64,128]{2,1,0:T(8,128)} %param.6) | copy-start | bytes 6291460
  11.4 5.4 %copy-start.8 = (f32[64,128]{1,0:T(8,128)S(1)}, f32[64,128]{1,0:T(8,128)}, u32[]{:S(2)}) copy-start(f32[64,128]{1,0:T(8,128)} %param.7) | copy-start | bytes 98308
  11.4 4.1 collective-permute-start.1
  22.2 6.6 %collective-permute-start.2 = (f32[64,1,128]{2,0,1:T(8,128)S(1)}, f32[64,1,128]{2,0,1:T(8,128)S(1)}, u32[]{:S(2)}, u32[]{:S(2)}) collective-permute-start(f32[64,1,128]{2,0,1:T(8,128)S(1)} %get-tuple-element.37), channel_id=1, source_target_pairs={{4,0},{8,4},{12,8},{16,12},{20,16},{24,20},{28,24},{5,1},{9,5},{13... | collective-permute-start | bytes 98312 | tf_op jit(solution)/shard_map/ppermute | solution.py:21
  23.5 6.1 %collective-permute-start.3 = (f32[64,1,128]{2,0,1:T(8,128)S(1)}, f32[64,1,128]{2,0,1:T(8,128)S(1)}, u32[]{:S(2)}, u32[]{:S(2)}) collective-permute-start(f32[64,1,128]{2,0,1:T(8,128)S(1)} %get-tuple-element.36), channel_id=1, source_target_pairs={{0,4},{4,8},{8,12},{12,16},{16,20},{20,24},{24,28},{1,5},{5,9},{9,... | collective-permute-start | bytes 98312 | tf_op jit(solution)/shard_map/ppermute | solution.py:20
  32.8 6.3 %collective-permute-start.4 = (f32[64,1,128]{2,0,1:T(8,128)S(1)}, f32[64,1,128]{2,0,1:T(8,128)S(1)}, u32[]{:S(2)}, u32[]{:S(2)}) collective-permute-start(f32[64,1,128]{2,0,1:T(8,128)S(1)} %get-tuple-element.35), channel_id=1, source_target_pairs={{4,0},{8,4},{12,8},{16,12},{20,16},{24,20},{28,24},{5,1},{9,5},{13... | collective-permute-start | bytes 98312 | tf_op jit(solution)/shard_map/ppermute | solution.py:21
  34.1 5.9 %collective-permute-start.5 = (f32[64,1,128]{2,0,1:T(8,128)S(1)}, f32[64,1,128]{2,0,1:T(8,128)S(1)}, u32[]{:S(2)}, u32[]{:S(2)}) collective-permute-start(f32[64,1,128]{2,0,1:T(8,128)S(1)} %get-tuple-element.34), channel_id=1, source_target_pairs={{0,4},{4,8},{8,12},{12,16},{16,20},{20,24},{24,28},{1,5},{5,9},{9,... | collective-permute-start | bytes 98312 | tf_op jit(solution)/shard_map/ppermute | solution.py:20
  43.0 6.3 %collective-permute-start.6 = (f32[64,1,128]{2,0,1:T(8,128)S(1)}, f32[64,1,128]{2,0,1:T(8,128)S(1)}, u32[]{:S(2)}, u32[]{:S(2)}) collective-permute-start(f32[64,1,128]{2,0,1:T(8,128)S(1)} %get-tuple-element.33), channel_id=1, source_target_pairs={{4,0},{8,4},{12,8},{16,12},{20,16},{24,20},{28,24},{5,1},{9,5},{13... | collective-permute-start | bytes 98312 | tf_op jit(solution)/shard_map/ppermute | solution.py:21
  44.3 5.9 %collective-permute-start.7 = (f32[64,1,128]{2,0,1:T(8,128)S(1)}, f32[64,1,128]{2,0,1:T(8,128)S(1)}, u32[]{:S(2)}, u32[]{:S(2)}) collective-permute-start(f32[64,1,128]{2,0,1:T(8,128)S(1)} %get-tuple-element.32), channel_id=1, source_target_pairs={{0,4},{4,8},{8,12},{12,16},{16,20},{20,24},{24,28},{1,5},{5,9},{9,... | collective-permute-start | bytes 98312 | tf_op jit(solution)/shard_map/ppermute | solution.py:20
  126.7 2.2 copy-start
  128.0 6.1 %copy-start.2 = (f32[64,4,16,128]{3,2,0,1:T(8,128)}, f32[64,4,16,128]{3,2,0,1:T(8,128)S(1)}, u32[]{:S(2)}) copy-start(f32[64,4,16,128]{3,2,0,1:T(8,128)S(1)} %copy.24) | copy-start | bytes 6291460
  134.1 172.5 %all-reduce.11.cloned.1.call-start = ((), (), s32[]{:S(2)}) async-start(), calls=%async_computation.2 | async-start | bytes 524288 | tf_op jit(solution)/shard_map/psum | solution.py:66
  272.1 90.8 %all-reduce.13.cloned.1.call-start = ((), (), s32[]{:S(2)}) async-start(), calls=%async_computation.3 | async-start | bytes 524288 | tf_op jit(solution)/shard_map/psum | solution.py:66
  363.9 39.6 %copy-start.6 = (f32[512,256]{0,1:T(8,128)S(1)}, f32[512,256]{0,1:T(8,128)}, u32[]{:S(2)}) copy-start(f32[512,256]{0,1:T(8,128)} %all-reduce.9.cloned.1.call-done) | copy-start | bytes 1572868
  401.0 2.6 copy-start.4
  403.5 2.1 copy-start.7
  430.4 2.2 copy-start.1
Sparse Core Ops, SparseCore 0:
  134.2 128.2 all-reduce.8
  272.2 34.3 all-reduce.10
  309.6 53.2 all-reduce.12
